TPU v7x, 32 devices: a whole 2x2x4 slice. The times are simulated.
32 devices in a mesh: row: 4 (over x, core), col: 2 (over y), store: 4 (over z).
Axes of the slice: x: 2, y: 2, z: 4, core: 2. Of those that a mesh axis runs over, the one named last changes fastest.
Arguments:
- hidden: bfloat16 [128, 128, 4096], P('store', 'row', 'col'), may hold values from -6 to 6
- out_grads: bfloat16 [208, 128, 128], P('row', 'store'), may hold values from -6 to 6
- proj_out: bfloat16 [208, 64], P('row'), may hold values from -0.4375 to 0.4375
- proj_in: bfloat16 [4096, 64], P('col'), may hold values from -0.09375 to 0.09375
- lengths: int32 [128], P('store'), may hold values from 64 to 128
- precond: bfloat16 [4096, 4096], P(('row', 'col'), 'store'), may hold values from -1 to 2, as said below
- stored: bfloat16 [12288, 4096], P(('row', 'col', 'store')), may hold values from -0.09375 to 0.09375
Outputs:
- scores: float32 [128, 12288], P(None, ('row', 'col', 'store'))
Inputs may be any that keep to these rules, and one draw needn't show every extreme that they name: Query q's live tokens are its first lengths[q] token slots. precond is symmetric.
All inputs are finite; a program needn't handle non-finite values.
Results may differ from a plain program's by a relative error of at most 0.0057.
Values may be sent and summed in bfloat16 or wider, within the bound.
No kernel may reach another device: no remote copies, remote signals or barrier semaphores. Data moves between devices by JAX's collectives and lax.ppermute only.
A program may use at most 64 MiB of HBM per device.

v0:
```python
import jax
import jax.numpy as jnp
from jax import lax
from jax.sharding import PartitionSpec as P

TOK = 128


def on_device(hidden, out_grads, proj_out, proj_in, lengths, precond, stored):
    queries, token_part, columns = hidden.shape
    width_in = proj_in.shape[1]
    local_proj = jnp.einsum(
        "qtc,cb->qtb", hidden, proj_in, preferred_element_type=jnp.float32
    ).astype(jnp.bfloat16)
    flattened = local_proj.reshape(queries, token_part * width_in)
    inputs_all = lax.all_gather(flattened, "row", axis=1, tiled=True).reshape(queries, -1, width_in)
    tokens = inputs_all.shape[1]
    position = jnp.arange(tokens, dtype=jnp.int32)
    live_mask = (position[None, :] < lengths[:, None]).astype(jnp.float32)
    outputs_proj = jnp.einsum(
        "rqt,ra->qta", out_grads, proj_out, preferred_element_type=jnp.float32
    )
    outputs_proj = (outputs_proj * live_mask[:, :, None]).astype(jnp.bfloat16)
    partial_value = jnp.einsum(
        "qta,qtb->qab", outputs_proj, inputs_all, preferred_element_type=jnp.float32
    )
    partial_value = partial_value.reshape(queries, -1) * TOK ** (-0.5)
    shares = lax.psum_scatter(
        partial_value, ("row", "col"), scatter_dimension=1, tiled=True
    ).astype(jnp.bfloat16)
    cond_terms = jnp.dot(
        shares,
        lax.all_gather(precond, "store", axis=1, tiled=True),
        preferred_element_type=jnp.float32,
    )
    conditioned = lax.psum_scatter(
        cond_terms, ("row", "col"), scatter_dimension=1, tiled=True
    ).astype(jnp.bfloat16)
    full_features = lax.all_gather(conditioned, ("row", "col"), axis=1, tiled=True)
    return lax.dot_general(
        lax.all_gather(full_features, "store", axis=0, tiled=True),
        stored,
        (((1,), (1,)), ((), ())),
        preferred_element_type=jnp.float32,
    )


def solution(mesh):
    return jax.shard_map(
        on_device,
        mesh=mesh,
        in_specs=(
            P("store", "row", "col"),
            P("row", "store", None),
            P("row", None),
            P("col", None),
            P("store"),
            P(("row", "col"), "store"),
            P(("row", "col", "store"), None),
        ),
        out_specs=P(None, ("row", "col", "store")),
        check_vma=False,
    )
```

profile of v0, /device:TPU:0, one launch (start us, length us, event | category | flops | bytes accessed | tf_op | source)
XLA Modules:
  0.0 207.3 jit_solution(10469774446894021144)
XLA Ops:
  7.4 0.0 reduce-scatter.3.cloned.1.call-start
  7.4 3.6 %convolution_convert_fusion = bf16[32,32,64]{2,1,0:T(8,128)(2,1)S(1)} fusion(bf16[32,32,2048]{2,1,0:T(8,128)(2,1)} %param.7, bf16[2048,64]{0,1:T(8,128)(2,1)} %param.10), kind=kOutput, calls=%fused_computation.3 | convolution fusion | flops 268500992 | bytes 4587520 | tf_op jit(solution)/shard_map/qtc,cb->qtb/dot_general | solution.py:12
  11.0 0.3 reshape.31
  11.3 9.1 %all_gather.12 = bf16[32,8192]{1,0:T(8,128)(2,1)} all-gather(bf16[32,2048]{1,0:T(8,128)(2,1)S(1)} %reshape.31), channel_id=1, replica_groups=mesh['row'=4,'col'=2,'store'=4] {'row'}, dimensions={1}, use_global_device_ids=true | all-gather | bytes 655360 | tf_op jit(solution)/shard_map/all_gather | solution.py:16
  20.3 2.7 %reshape.32 = bf16[32,128,64]{2,1,0:T(8,128)(2,1)} reshape(bf16[32,8192]{1,0:T(8,128)(2,1)} %all_gather.12) | data formatting | bytes 1048576 | tf_op jit(solution)/shard_map/reshape | solution.py:16
  23.1 0.7 fusion.7
  23.8 0.0 copy-done.1
  23.8 3.0 %convolution_multiply_fusion.1 = f32[32,64,64]{2,1,0:T(8,128)} fusion(bf16[32,128,64]{2,1,0:T(8,128)(2,1)} %reshape.32, f32[32,128]{1,0:T(8,128)S(1)} %fusion.7, bf16[52,32,128]{2,1,0:T(8,128)(2,1)} %param.8, bf16[52,64]{1,0:T(8,128)(2,1)S(1)} %copy-done.1), kind=kOutput, calls=%fused_computation.1 | convolution fusion | flops 61472768 | bytes 1497600 | tf_op jit(solution)/shard_map/qta,qtb->qab/dot_general | solution.py:24
  26.8 2.4 %mul.21 = f32[32,4096]{1,0:T(8,128)} reshape(f32[32,64,64]{2,1,0:T(8,128)} %convolution_multiply_fusion.1) | data formatting | bytes 1048576 | tf_op jit(solution)/shard_map/mul | solution.py:27
  29.2 0.0 reduce-scatter.3.cloned.1.call-update
  29.3 0.0 all-gather.3.cloned.1.call-start
  29.3 0.5 all-gather.3.cloned.1.call-update
  29.8 0.0 reduce-scatter.5.cloned.1.call-start
  29.9 34.5 %reduce-scatter.3.cloned.1.call-done = f32[32,512]{1,0:T(8,128)} async-done(((f32[32,4096]{1,0:T(8,128)}), f32[32,512]{1,0:T(8,128)}) %reduce-scatter.3.cloned.1.call-update) | async-done | bytes 65552 | tf_op jit(solution)/shard_map/reduce_scatter | solution.py:28
  64.4 48.4 %all-gather.3.cloned.1.call-done = bf16[512,4096]{1,0:T(8,128)(2,1)} async-done(((bf16[512,1024]{1,0:T(8,128)(2,1)}), bf16[512,4096]{1,0:T(8,128)(2,1)}) %all-gather.3.cloned.1.call-update) | async-done | bytes 4194320 | tf_op jit(solution)/shard_map/all_gather | solution.py:33
  112.8 3.9 %fusion.5 = f32[32,4096]{1,0:T(8,128)} fusion(bf16[512,4096]{1,0:T(8,128)(2,1)} %all-gather.3.cloned.1.call-done, f32[32,512]{1,0:T(8,128)} %reduce-scatter.3.cloned.1.call-done), kind=kOutput, calls=%fused_computation.7 | convolution fusion | flops 134234112 | bytes 4784128 | tf_op jit(solution)/shard_map/dot_general | solution.py:31
  116.7 0.0 reduce-scatter.5.cloned.1.call-update
  116.7 0.0 all-gather.5.cloned.1.call-start
  116.7 32.7 %reduce-scatter.5.cloned.1.call-done = f32[32,512]{1,0:T(8,128)} async-done(((f32[32,4096]{1,0:T(8,128)}), f32[32,512]{1,0:T(8,128)}) %reduce-scatter.5.cloned.1.call-update) | async-done | bytes 65552 | tf_op jit(solution)/shard_map/reduce_scatter | solution.py:36
  149.4 0.8 convert_element_type.23
  150.3 18.6 %all_gather.14 = bf16[32,4096]{1,0:T(8,128)(2,1)} all-gather(bf16[32,512]{1,0:T(8,128)(2,1)S(1)} %convert_element_type.23), channel_id=1, replica_groups=mesh['row'=4,'col'=2,'store'=4] {'row','col'}, dimensions={1}, use_global_device_ids=true | all-gather | bytes 294912 | tf_op jit(solution)/shard_map/all_gather | solution.py:39
  168.9 0.0 all-gather.5.cloned.1.call-update
  168.9 28.0 %all-gather.5.cloned.1.call-done = bf16[128,4096]{1,0:T(8,128)(2,1)} async-done(((bf16[32,4096]{1,0:T(8,128)(2,1)}), bf16[128,4096]{1,0:T(8,128)(2,1)}) %all-gather.5.cloned.1.call-update) | async-done | bytes 1048592 | tf_op jit(solution)/shard_map/all_gather | solution.py:41
  196.9 3.0 %fusion.10 = f32[128,384]{1,0:T(8,128)} fusion(bf16[128,4096]{1,0:T(8,128)(2,1)} %all-gather.5.cloned.1.call-done, bf16[384,4096]{1,0:T(8,128)(2,1)S(1)} %copy-done), kind=kOutput, calls=%fused_computation.12 | convolution fusion | flops 402653184 | bytes 4390912 | tf_op jit(solution)/shard_map/dot_general | solution.py:40
  (3 shorter events, 0.0 us)
Async XLA Ops:
  7.4 189.6 %copy-start = (bf16[384,4096]{1,0:T(8,128)(2,1)S(1)}, bf16[384,4096]{1,0:T(8,128)(2,1)}, u32[]{:S(2)}) copy-start(bf16[384,4096]{1,0:T(8,128)(2,1)} %param.13) | copy-start | bytes 9437188
  7.4 16.5 %copy-start.1 = (bf16[52,64]{1,0:T(8,128)(2,1)S(1)}, bf16[52,64]{1,0:T(8,128)(2,1)}, u32[]{:S(2)}) copy-start(bf16[52,64]{1,0:T(8,128)(2,1)} %param.9) | copy-start | bytes 19972
  7.4 57.0 %reduce-scatter.3.cloned.1.call-start = ((), (), s32[]{:S(2)}) async-start(), calls=%async_computation.2 | async-start | bytes 589824 | tf_op jit(solution)/shard_map/reduce_scatter | solution.py:28
  29.3 83.5 %all-gather.3.cloned.1.call-start = ((), (), s32[]{:S(2)}) async-start(), calls=%async_computation.3 | async-start | bytes 5242880 | tf_op jit(solution)/shard_map/all_gather | solution.py:33
  29.8 119.6 %reduce-scatter.5.cloned.1.call-start = ((), (), s32[]{:S(2)}) async-start(), calls=%async_computation.4 | async-start | bytes 589824 | tf_op jit(solution)/shard_map/reduce_scatter | solution.py:36
  116.7 80.2 %all-gather.5.cloned.1.call-start = ((), (), s32[]{:S(2)}) async-start(), calls=%async_computation.5 | async-start | bytes 1310720 | tf_op jit(solution)/shard_map/all_gather | solution.py:41
Sparse Core Ops, SparseCore 0:
  29.4 34.9 reduce-scatter.2
  116.8 32.5 reduce-scatter.4
Sparse Core Ops, SparseCore 1:
  31.3 81.4 all-gather.2
  169.0 27.9 all-gather.4
where the time goes:
time: 208 us; the launch traced here: 207 us
  waiting for transfers between devices  144 us (69%)
  blocking collectives  27.7 us (13%)
  between operations  14.9 us (7%)
  matrix products  13.4 us (6%)
  local copies, waits for them, and re-layouts  5.42 us (3%)
    all_gather x1, waiting for transfers between devices, on_device(): lax.all_gather(precond, 'store', axis=1, tiled=True)  48.4 us
    reduce_scatter x1, waiting for transfers between devices, on_device(): lax.psum_scatter(partial_value, ('row', 'col'), scatter_dimension=1, tile...  34.5 us
    reduce_scatter x1, waiting for transfers between devices, on_device(): lax.psum_scatter(cond_terms, ('row', 'col'), scatter_dimension=1, tiled=T...  32.7 us
    all_gather x1, waiting for transfers between devices, on_device(): lax.all_gather(full_features, 'store', axis=0, tiled=True)  28 us
    all_gather x1, blocking collectives, on_device(): lax.all_gather(conditioned, ('row', 'col'), axis=1, tiled=True)  18.6 us
    all_gather x1, blocking collectives, on_device(): lax.all_gather(flattened, 'row', axis=1, tiled=True)  9.09 us
  transfers between devices with their start and end apart: 4, of which 4 were waited for; matrix products, arithmetic and copies ran while one was open for 0% of the time, Pallas kernels for 0%

commit v1 on v0

--- a/solution.py
+++ b/solution.py
@@ -4,6 +4,10 @@
 from jax.sharding import PartitionSpec as P
 
 TOK = 128
+
+
+def load_entries_on(array_here):
+    return jnp.concatenate(lax.all_gather(array_here, "store"), 1)
 
 
 def on_device(hidden, out_grads, proj_out, proj_in, lengths, precond, stored):
@@ -28,11 +32,7 @@
     shares = lax.psum_scatter(
         partial_value, ("row", "col"), scatter_dimension=1, tiled=True
     ).astype(jnp.bfloat16)
-    cond_terms = jnp.dot(
-        shares,
-        lax.all_gather(precond, "store", axis=1, tiled=True),
-        preferred_element_type=jnp.float32,
-    )
+    cond_terms = jnp.dot(shares, load_entries_on(precond), preferred_element_type=jnp.float32)
     conditioned = lax.psum_scatter(
         cond_terms, ("row", "col"), scatter_dimension=1, tiled=True
     ).astype(jnp.bfloat16)

time: 208 us -> 195 us (0.938)
  waiting for transfers between devices: 144 us -> 125 us
  local copies, waits for them, and re-layouts: 5.42 us -> 11.7 us
    reduce_scatter x1, waiting for transfers between devices: 34.5 us -> 0.01 us  [on_device(): lax.psum_scatter(partial_value, ('row', 'col'), scatter_dimension=1, tile...]
    all_gather x1, waiting for transfers between devices: 48.4 us -> 63.2 us  [load_entries_on(): return jnp.concatenate(lax.all_gather(array_here, 'store'), 1)]
    reshape x0 -> x1, local copies, waits for them, and re-layouts: none -> 6.25 us  [load_entries_on(): return jnp.concatenate(lax.all_gather(array_here, 'store'), 1)]
  transfers between devices with their start and end apart: 4 -> 4, of which waited for: 4 -> 3; matrix products, arithmetic and copies ran while one was open for 0% -> 10% of each run, Pallas kernels for 0% -> 0%
where the time goes in v1:
time: 195 us
  waiting for transfers between devices  125 us (64%)
  blocking collectives  27.7 us (14%)
  between operations  14.9 us (8%)
  matrix products  13.9 us (7%)
  local copies, waits for them, and re-layouts  11.7 us (6%)
    all_gather x1, waiting for transfers between devices, load_entries_on(): return jnp.concatenate(lax.all_gather(array_here, 'store'), 1)  63.2 us
    reduce_scatter x1, waiting for transfers between devices, on_device(): lax.psum_scatter(cond_terms, ('row', 'col'), scatter_dimension=1, tiled=T...  32.6 us
    all_gather x1, waiting for transfers between devices, on_device(): lax.all_gather(full_features, 'store', axis=0, tiled=True)  28.2 us
    all_gather x1, blocking collectives, on_device(): lax.all_gather(conditioned, ('row', 'col'), axis=1, tiled=True)  18.6 us
    all_gather x1, blocking collectives, on_device(): lax.all_gather(flattened, 'row', axis=1, tiled=True)  9.09 us
    reshape x1, local copies, waits for them, and re-layouts, load_entries_on(): return jnp.concatenate(lax.all_gather(array_here, 'store'), 1)  6.25 us
    dot_general x1, matrix products, on_device(): jnp.dot(shares, load_entries_on(precond), preferred_element_type=jnp.floa...  4.36 us
  transfers between devices with their start and end apart: 4, of which 3 were waited for; matrix products, arithmetic and copies ran while one was open for 10% of the time, Pallas kernels for 0%

profile of v1, /device:TPU:0, one launch (start us, length us, event | category | flops | bytes accessed | tf_op | source)
XLA Modules:
  0.0 194.6 jit_solution(18022620711826235463)
XLA Ops:
  7.4 0.0 copy-start
  7.4 0.0 all-gather.6.cloned.1.call-start
  7.4 0.7 all-gather.6.cloned.1.call-update
  8.1 0.0 reduce-scatter.3.cloned.1.call-start
  8.1 3.6 %convolution_convert_fusion = bf16[32,32,64]{2,1,0:T(8,128)(2,1)S(1)} fusion(bf16[32,32,2048]{2,1,0:T(8,128)(2,1)} %param.7, bf16[2048,64]{0,1:T(8,128)(2,1)} %param.10), kind=kOutput, calls=%fused_computation.3 | convolution fusion | flops 268500992 | bytes 4587520 | tf_op jit(solution)/shard_map/qtc,cb->qtb/dot_general | solution.py:16
  11.7 0.3 reshape.37
  12.0 9.1 %all_gather.15 = bf16[32,8192]{1,0:T(8,128)(2,1)} all-gather(bf16[32,2048]{1,0:T(8,128)(2,1)S(1)} %reshape.37), channel_id=1, replica_groups=mesh['row'=4,'col'=2,'store'=4] {'row'}, dimensions={1}, use_global_device_ids=true | all-gather | bytes 655360 | tf_op jit(solution)/shard_map/all_gather | solution.py:20
  21.1 2.7 %reshape.38 = bf16[32,128,64]{2,1,0:T(8,128)(2,1)} reshape(bf16[32,8192]{1,0:T(8,128)(2,1)} %all_gather.15) | data formatting | bytes 1048576 | tf_op jit(solution)/shard_map/reshape | solution.py:20
  23.9 0.7 fusion.7
  24.6 3.0 %convolution_multiply_fusion.1 = f32[32,64,64]{2,1,0:T(8,128)} fusion(bf16[32,128,64]{2,1,0:T(8,128)(2,1)} %reshape.38, f32[32,128]{1,0:T(8,128)S(1)} %fusion.7, bf16[52,32,128]{2,1,0:T(8,128)(2,1)} %param.8, bf16[52,64]{1,0:T(8,128)(2,1)S(1)} %copy-done.1), kind=kOutput, calls=%fused_computation.1 | convolution fusion | flops 61472768 | bytes 1497600 | tf_op jit(solution)/shard_map/qta,qtb->qab/dot_general | solution.py:28
  27.6 2.4 %mul.21 = f32[32,4096]{1,0:T(8,128)} reshape(f32[32,64,64]{2,1,0:T(8,128)} %convolution_multiply_fusion.1) | data formatting | bytes 1048576 | tf_op jit(solution)/shard_map/mul | solution.py:31
  30.0 0.0 reduce-scatter.3.cloned.1.call-update
  30.0 0.0 reduce-scatter.5.cloned.1.call-start
  30.1 63.2 %all-gather.6.cloned.1.call-done = bf16[2048,1024]{1,0:T(8,128)(2,1)} async-done(((bf16[512,1024]{1,0:T(8,128)(2,1)}), bf16[2048,1024]{1,0:T(8,128)(2,1)}) %all-gather.6.cloned.1.call-update) | async-done | bytes 4194320 | tf_op jit(solution)/shard_map/all_gather | solution.py:10
  93.2 6.3 %copy.11 = bf16[512,4,1024]{0,2,1:T(8,128)(2,1)} copy(bf16[512,4,1024]{2,0,1:T(8,128)(2,1)} %bitcast.17) | data formatting | bytes 8388608 | tf_op jit(solution)/shard_map/reshape | solution.py:10
  99.5 4.4 %fusion.5 = f32[32,4096]{1,0:T(8,128)} fusion(bf16[512,4096]{0,1:T(8,128)(2,1)} %bitcast.16, f32[32,512]{1,0:T(8,128)} %reduce-scatter.3.cloned.1.call-done), kind=kOutput, calls=%fused_computation.7 | convolution fusion | flops 134234112 | bytes 4784128 | tf_op jit(solution)/shard_map/dot_general | solution.py:35
  103.8 0.0 reduce-scatter.5.cloned.1.call-update
  103.9 0.0 all-gather.4.cloned.1.call-start
  103.9 32.6 %reduce-scatter.5.cloned.1.call-done = f32[32,512]{1,0:T(8,128)} async-done(((f32[32,4096]{1,0:T(8,128)}), f32[32,512]{1,0:T(8,128)}) %reduce-scatter.5.cloned.1.call-update) | async-done | bytes 65552 | tf_op jit(solution)/shard_map/reduce_scatter | solution.py:36
  136.6 0.8 convert_element_type.23
  137.4 18.6 %all_gather.18 = bf16[32,4096]{1,0:T(8,128)(2,1)} all-gather(bf16[32,512]{1,0:T(8,128)(2,1)S(1)} %convert_element_type.23), channel_id=1, replica_groups=mesh['row'=4,'col'=2,'store'=4] {'row','col'}, dimensions={1}, use_global_device_ids=true | all-gather | bytes 294912 | tf_op jit(solution)/shard_map/all_gather | solution.py:39
  156.0 0.0 all-gather.4.cloned.1.call-update
  156.0 28.2 %all-gather.4.cloned.1.call-done = bf16[128,4096]{1,0:T(8,128)(2,1)} async-done(((bf16[32,4096]{1,0:T(8,128)(2,1)}), bf16[128,4096]{1,0:T(8,128)(2,1)}) %all-gather.4.cloned.1.call-update) | async-done | bytes 1048592 | tf_op jit(solution)/shard_map/all_gather | solution.py:41
  184.2 3.0 %fusion.10 = f32[128,384]{1,0:T(8,128)} fusion(bf16[128,4096]{1,0:T(8,128)(2,1)} %all-gather.4.cloned.1.call-done, bf16[384,4096]{1,0:T(8,128)(2,1)S(1)} %copy-done), kind=kOutput, calls=%fused_computation.12 | convolution fusion | flops 402653184 | bytes 4390912 | tf_op jit(solution)/shard_map/dot_general | solution.py:40
  (4 shorter events, 0.0 us)
Async XLA Ops:
  7.4 176.8 %copy-start = (bf16[384,4096]{1,0:T(8,128)(2,1)S(1)}, bf16[384,4096]{1,0:T(8,128)(2,1)}, u32[]{:S(2)}) copy-start(bf16[384,4096]{1,0:T(8,128)(2,1)} %param.13) | copy-start | bytes 9437188
  7.4 17.2 %copy-start.1 = (bf16[52,64]{1,0:T(8,128)(2,1)S(1)}, bf16[52,64]{1,0:T(8,128)(2,1)}, u32[]{:S(2)}) copy-start(bf16[52,64]{1,0:T(8,128)(2,1)} %param.9) | copy-start | bytes 19972
  7.4 85.9 %all-gather.6.cloned.1.call-start = ((), (), s32[]{:S(2)}) async-start(), calls=%async_computation.5 | async-start | bytes 5242880 | tf_op jit(solution)/shard_map/all_gather | solution.py:10
  8.1 91.4 %reduce-scatter.3.cloned.1.call-start = ((), (), s32[]{:S(2)}) async-start(), calls=%async_computation.2 | async-start | bytes 589824 | tf_op jit(solution)/shard_map/reduce_scatter | solution.py:32
  30.0 106.5 %reduce-scatter.5.cloned.1.call-start = ((), (), s32[]{:S(2)}) async-start(), calls=%async_computation.3 | async-start | bytes 589824 | tf_op jit(solution)/shard_map/reduce_scatter | solution.py:36
  103.9 80.3 %all-gather.4.cloned.1.call-start = ((), (), s32[]{:S(2)}) async-start(), calls=%async_computation.4 | async-start | bytes 1310720 | tf_op jit(solution)/shard_map/all_gather | solution.py:41
Sparse Core Ops, SparseCore 0:
  9.7 83.4 all-gather.5
  156.2 27.9 all-gather.3
Sparse Core Ops, SparseCore 1:
  30.1 34.9 reduce-scatter.2
  104.0 32.5 reduce-scatter.4
